TPU v7x, 32 devices: a whole 2x2x4 slice. The times are simulated.
32 devices in a mesh: freq: 16 (over z, x, core), rcv: 2 (over y).
Axes of the slice: x: 2, y: 2, z: 4, core: 2. Of those that a mesh axis runs over, the one named last changes fastest.
Arguments:
- reflection: bfloat16 [2, 128, 768, 768], P(None, 'freq', 'rcv'), may hold values from -0.21875 to 0.21875
- direct: bfloat16 [768, 128, 512], P(('rcv', 'freq')), may hold values from -6 to 6
- onset: int32 [768, 128], P(('rcv', 'freq')), may hold values from 128 to 383
Outputs:
- focus_plus: bfloat16 [768, 128, 512], P(('rcv', 'freq'))
- focus_minus: bfloat16 [768, 128, 512], P(('rcv', 'freq'))
- correlation: float32 [2, 128, 128, 128], P(None, 'freq', 'rcv')
All inputs are finite; a program needn't handle non-finite values.
Results may differ from a plain program's by a relative error of at most 0.019.
Values may be sent and summed in bfloat16 or wider, within the bound.
A program may use at most 64 MiB of HBM per device.

v0:
```python
import math

import jax
import jax.numpy as jnp
from jax import lax
from jax.sharding import PartitionSpec as P


def lookup_tables(samples, frequencies):
    sample = jnp.arange(samples, dtype=jnp.int32)
    spectral_bin_index = jnp.arange(frequencies, dtype=jnp.int32)
    phase_index = sample[:, None] * spectral_bin_index[None, :] % samples
    angles = 2.0 * math.pi / samples * phase_index.astype(jnp.float32)
    cosine = jnp.cos(angles)
    sine = jnp.sin(angles)
    forward = (jnp.stack([cosine, -sine], axis=1) / math.sqrt(samples)).astype(jnp.bfloat16)
    inverse = (jnp.stack([cosine.T, -sine.T], axis=0) * (2.0 / math.sqrt(samples))).astype(
        jnp.bfloat16
    )
    return (forward, inverse)


def fourier_spectrum(field, forward):
    local_spectra = jnp.einsum(
        "sqt,tcf->scfq", field, forward, preferred_element_type=jnp.float32
    ).astype(jnp.bfloat16)
    return lax.all_to_all(local_spectra, "freq", split_axis=2, concat_axis=0, tiled=True)


def make_term(spectra, reflection, conj_sign):
    spectrum_real_rows = spectra[:, 0]
    spec_imag = spectra[:, 1]

    def product(left_operand, right_operand):
        return jnp.einsum(
            "key,ekn->ykn", left_operand, right_operand, preferred_element_type=jnp.float32
        )

    real_part = product(reflection[0], spectrum_real_rows) - conj_sign * product(
        reflection[1], spec_imag
    )
    imag_part = product(reflection[0], spec_imag) + conj_sign * product(
        reflection[1], spectrum_real_rows
    )
    return jnp.stack([real_part, imag_part], axis=1)


def to_time(spectra, reflection, conj_sign):
    summed = lax.psum_scatter(
        make_term(spectra, reflection, conj_sign).astype(jnp.bfloat16),
        "rcv",
        scatter_dimension=0,
        tiled=True,
    )
    return lax.all_to_all(summed, "freq", split_axis=0, concat_axis=2, tiled=True)


def inverse_window(summed, onset, inverse):
    traces = jnp.einsum("scfq,cft->sqt", summed, inverse, preferred_element_type=jnp.float32)
    sample = jnp.arange(traces.shape[2], dtype=jnp.int32)
    window = (sample[None, None, :] < onset[:, :, None]).astype(jnp.float32)
    return traces * window


def on_device(reflection, direct, onset):
    samples = direct.shape[2]
    frequencies = reflection.shape[1] * lax.axis_size("freq")
    forward, inverse = lookup_tables(samples, frequencies)
    focus_plus = direct
    minus_spectrum = None
    plus_spectrum = fourier_spectrum(focus_plus, forward)
    focus_minus = inverse_window(to_time(plus_spectrum, reflection, 1.0), onset, inverse).astype(
        jnp.bfloat16
    )
    minus_spectrum = fourier_spectrum(focus_minus, forward)
    returned = inverse_window(to_time(minus_spectrum, reflection, -1.0), onset, inverse)
    focus_plus = (direct.astype(jnp.float32) + returned).astype(jnp.bfloat16)
    plus_spectrum = fourier_spectrum(focus_plus, forward)
    receivers = reflection.shape[3]
    summed = lax.psum_scatter(
        make_term(plus_spectrum, reflection, 1.0).astype(jnp.bfloat16),
        "rcv",
        scatter_dimension=0,
        tiled=True,
    ).astype(jnp.float32)
    green_field = (summed - minus_spectrum.astype(jnp.float32)).astype(jnp.bfloat16)
    green_real = green_field[:, 0]
    green_imag = green_field[:, 1]

    def pairwise(left_operand, right_operand):
        return jnp.einsum(
            "rfa,rfb->fab", left_operand, right_operand, preferred_element_type=jnp.float32
        )

    real_part = pairwise(green_real, green_real) + pairwise(green_imag, green_imag)
    imag_part = pairwise(green_real, green_imag) - pairwise(green_imag, green_real)
    partial_corr = jnp.stack([real_part, imag_part], axis=0) / receivers
    correlation = lax.psum_scatter(
        partial_corr.astype(jnp.bfloat16), "rcv", scatter_dimension=2, tiled=True
    ).astype(jnp.float32)
    return (focus_plus, focus_minus, correlation)


def solution(mesh):
    placed = (
        P(None, "freq", "rcv", None),
        P(("rcv", "freq"), None, None),
        P(("rcv", "freq"), None),
    )
    return jax.shard_map(
        on_device,
        mesh=mesh,
        in_specs=placed,
        out_specs=(
            P(("rcv", "freq"), None, None),
            P(("rcv", "freq"), None, None),
            P(None, "freq", "rcv", None),
        ),
        check_vma=False,
    )
```

profile of v0, /device:TPU:28, one launch (start us, length us, event | category | flops | bytes accessed | tf_op | source)
XLA Modules:
  0.0 448.6 jit_solution(11347664271392090336)
XLA Ops:
  8.3 3.0 fusion.94
  12.3 40.3 %all_to_all.90 = bf16[24,2,128,128]{3,0,1,2:T(8,128)(2,1)S(1)} all-to-all(bf16[24,2,128,128]{3,0,1,2:T(8,128)(2,1)S(1)} %copy.56), channel_id=1, replica_groups=mesh['freq'=16,'rcv'=2] {'freq'}, dimensions={2} | all-to-all | bytes 3145728 | tf_op jit(solution)/shard_map/all_to_all | solution.py:27
  54.3 3.5 fusion.11
  57.8 3.7 fusion.13
  64.0 2.9 copy.101
  66.9 44.1 %reduce-scatter.13.cloned.1.call-done = bf16[384,2048]{1,0:T(8,128)(2,1)} async-done(((bf16[768,2048]{1,0:T(8,128)(2,1)}), bf16[384,2048]{1,0:T(8,128)(2,1)}) %reduce-scatter.13.cloned.1.call-update) | async-done | bytes 1572880
  111.0 1.9 copy.102
  112.9 2.0 copy.61
  114.8 6.0 %all-to-all-start.1 = ((bf16[384,2,8,128]{3,2,1,0:T(8,128)(2,1)}), bf16[384,2,8,128]{3,2,1,0:T(8,128)(2,1)S(1)}, u32[]{:S(2)}, u32[]{:S(2)}) async-start(bf16[384,2,8,128]{3,2,1,0:T(8,128)(2,1)} %copy.61), calls=%async_computation.1 | async-start | bytes 3145728 | tf_op jit(solution)/shard_map/all_to_all | solution.py:55
  122.1 31.5 %all-to-all-done.1 = bf16[384,2,8,128]{3,2,1,0:T(8,128)(2,1)S(1)} async-done(((bf16[384,2,8,128]{3,2,1,0:T(8,128)(2,1)}), bf16[384,2,8,128]{3,2,1,0:T(8,128)(2,1)S(1)}, u32[]{:S(2)}, u32[]{:S(2)}) %all-to-all-start.1) | async-done | bytes 1572896 | tf_op jit(solution)/shard_map/all_to_all | solution.py:55
  157.2 42.4 %all_to_all.91 = bf16[24,2,128,128]{3,0,1,2:T(8,128)(2,1)S(1)} all-to-all(bf16[24,2,128,128]{3,0,1,2:T(8,128)(2,1)S(1)} %copy.64), channel_id=1, replica_groups=mesh['freq'=16,'rcv'=2] {'freq'}, dimensions={2} | all-to-all | bytes 3145728 | tf_op jit(solution)/shard_map/all_to_all | solution.py:27
  201.5 1.6 copy.109
  203.2 3.5 fusion.7
  206.7 3.7 fusion.9
  212.5 1.9 pad_maximum_fusion.1
  214.5 4.7 %copy.103 = bf16[768,2048]{1,0:T(8,128)(2,1)} copy(bf16[768,2048]{0,1:T(8,128)(2,1)} %bitcast.210) | data formatting | bytes 6291456
  219.2 44.0 %reduce-scatter.15.cloned.1.call-done = bf16[384,2048]{1,0:T(8,128)(2,1)} async-done(((bf16[768,2048]{1,0:T(8,128)(2,1)}), bf16[384,2048]{1,0:T(8,128)(2,1)}) %reduce-scatter.15.cloned.1.call-update) | async-done | bytes 1572880
  263.3 1.9 copy.104
  265.2 2.0 copy.69
  267.1 40.8 %all_to_all.92 = bf16[384,2,8,128]{3,2,1,0:T(8,128)(2,1)S(1)} all-to-all(bf16[384,2,8,128]{3,2,1,0:T(8,128)(2,1)} %copy.69), channel_id=1, replica_groups=mesh['freq'=16,'rcv'=2] {'freq'}, dimensions={0} | all-to-all | bytes 3145728 | tf_op jit(solution)/shard_map/all_to_all | solution.py:55
  307.9 2.8 fusion.1
  312.8 40.8 %all_to_all.93 = bf16[24,2,128,128]{3,0,1,2:T(8,128)(2,1)S(1)} all-to-all(bf16[24,2,128,128]{3,0,1,2:T(8,128)(2,1)S(1)} %copy.72), channel_id=1, replica_groups=mesh['freq'=16,'rcv'=2] {'freq'}, dimensions={2} | all-to-all | bytes 3145728 | tf_op jit(solution)/shard_map/all_to_all | solution.py:27
  357.2 3.5 fusion.3
  360.7 3.7 fusion.5
  366.6 2.0 pad_maximum_fusion.2
  368.5 4.7 %copy.105 = bf16[768,2048]{1,0:T(8,128)(2,1)} copy(bf16[768,2048]{0,1:T(8,128)(2,1)} %bitcast.211) | data formatting | bytes 6291456
  373.3 44.0 %reduce-scatter.17.cloned.1.call-done = bf16[384,2048]{1,0:T(8,128)(2,1)} async-done(((bf16[768,2048]{1,0:T(8,128)(2,1)}), bf16[384,2048]{1,0:T(8,128)(2,1)}) %reduce-scatter.17.cloned.1.call-update) | async-done | bytes 1572880
  417.3 1.9 copy.106
  419.2 1.7 copy.77
  420.9 1.9 subtract_convert_fusion
  425.5 14.8 %reduce-scatter.11.cloned.1.call-done = bf16[2,8,64,128]{3,2,1,0:T(8,128)(2,1)} async-done(((bf16[2,8,128,128]{3,2,1,0:T(8,128)(2,1)}), bf16[2,8,64,128]{3,2,1,0:T(8,128)(2,1)}) %reduce-scatter.11.cloned.1.call-update) | async-done | bytes 262160 | tf_op jit(solution)/shard_map/reduce_scatter | solution.py:98
  440.3 1.8 convert_element_type.103
  (78 shorter events, 25.6 us)
Async XLA Ops:
  7.2 103.8 %reduce-scatter.13.cloned.1.call-start = ((), (), s32[]{:S(2)}) async-start(), calls=%async_computation.10 | async-start | bytes 4718592
  8.3 4.1 copy-start
  54.3 7.2 %slice-start = ((s8[9437184]{0:T(1024)(128)(4,1)}), s8[4194304]{0:T(1024)(128)(4,1)S(1)}, s32[]{:S(2)}) async-start(s8[9437184]{0:T(1024)(128)(4,1)} %bitcast.201), calls=%async_computation.13 | async-start | bytes 8388608
  54.3 7.2 %slice-start.1 = ((s8[9437184]{0:T(1024)(128)(4,1)}), s8[4194304]{0:T(1024)(128)(4,1)S(1)}, s32[]{:S(2)}) async-start(s8[9437184]{0:T(1024)(128)(4,1)} %bitcast.201), calls=%async_computation.14 | async-start | bytes 8388608
  57.8 3.7 slice-start.2
  112.8 40.9 %copy-start.8 = (s32[24,128]{1,0:T(8,128)S(1)}, s32[24,128]{1,0:T(8,128)}, u32[]{:S(2)}) copy-start(s32[24,128]{1,0:T(8,128)} %param.5) | copy-start | bytes 36868
  114.8 38.9 %all-to-all-start.1 = ((bf16[384,2,8,128]{3,2,1,0:T(8,128)(2,1)}), bf16[384,2,8,128]{3,2,1,0:T(8,128)(2,1)S(1)}, u32[]{:S(2)}, u32[]{:S(2)}) async-start(bf16[384,2,8,128]{3,2,1,0:T(8,128)(2,1)} %copy.61), calls=%async_computation.1 | async-start | bytes 3145728 | tf_op jit(solution)/shard_map/all_to_all | solution.py:55
  120.9 142.4 %reduce-scatter.15.cloned.1.call-start = ((), (), s32[]{:S(2)}) async-start(), calls=%async_computation.11 | async-start | bytes 4718592
  122.1 33.0 %copy-start.6 = (f32[1,128,512]{2,1,0:T(8,128)}, f32[1,128,512]{2,1,0:T(8,128)S(1)}, u32[]{:S(2)}) copy-start(f32[1,128,512]{2,1,0:T(8,128)S(1)} %get-tuple-element.11) | copy-start | bytes 786436
  122.1 33.0 %copy-start.7 = (f32[1,128,512]{2,1,0:T(8,128)}, f32[1,128,512]{2,1,0:T(8,128)S(1)}, u32[]{:S(2)}) copy-start(f32[1,128,512]{2,1,0:T(8,128)S(1)} %get-tuple-element.12) | copy-start | bytes 786436
  153.7 1.4 copy-start.1
  155.1 2.1 copy-start.4
  203.1 7.2 %slice-start.3 = ((s8[9437184]{0:T(1024)(128)(4,1)}), s8[4194304]{0:T(1024)(128)(4,1)S(1)}, s32[]{:S(2)}) async-start(s8[9437184]{0:T(1024)(128)(4,1)} %bitcast.203), calls=%async_computation.16 | async-start | bytes 8388608
  203.2 7.2 %slice-start.4 = ((s8[9437184]{0:T(1024)(128)(4,1)}), s8[4194304]{0:T(1024)(128)(4,1)S(1)}, s32[]{:S(2)}) async-start(s8[9437184]{0:T(1024)(128)(4,1)} %bitcast.203), calls=%async_computation.17 | async-start | bytes 8388608
  206.6 3.7 slice-start.5
  219.2 198.1 %reduce-scatter.17.cloned.1.call-start = ((), (), s32[]{:S(2)}) async-start(), calls=%async_computation.12 | async-start | bytes 4718592
  267.1 40.8 %copy-start.3 = (bf16[24,128,512]{2,1,0:T(8,128)(2,1)S(1)}, bf16[24,128,512]{2,1,0:T(8,128)(2,1)}, u32[]{:S(2)}) copy-start(bf16[24,128,512]{2,1,0:T(8,128)(2,1)} %param.4) | copy-start | bytes 9437188
  307.9 2.8 copy-start.2
  310.7 2.1 copy-start.5
  357.2 7.2 %slice-start.6 = ((s8[9437184]{0:T(1024)(128)(4,1)}), s8[4194304]{0:T(1024)(128)(4,1)S(1)}, s32[]{:S(2)}) async-start(s8[9437184]{0:T(1024)(128)(4,1)} %bitcast.205), calls=%async_computation.19 | async-start | bytes 8388608
  357.2 7.2 %slice-start.7 = ((s8[9437184]{0:T(1024)(128)(4,1)}), s8[4194304]{0:T(1024)(128)(4,1)S(1)}, s32[]{:S(2)}) async-start(s8[9437184]{0:T(1024)(128)(4,1)} %bitcast.205), calls=%async_computation.20 | async-start | bytes 8388608
  360.6 3.7 slice-start.8
  373.2 67.1 %reduce-scatter.11.cloned.1.call-start = ((), (), s32[]{:S(2)}) async-start(), calls=%async_computation.9 | async-start | bytes 786432 | tf_op jit(solution)/shard_map/reduce_scatter | solution.py:98
Sparse Core Ops, SparseCore 0:
  67.0 43.9 reduce-scatter.12
  219.3 43.9 reduce-scatter.14
  373.3 43.9 reduce-scatter.16
  425.6 14.6 reduce-scatter.10
where the time goes:
time: 452 us; the launch traced here: 449 us
  waiting for transfers between devices  179 us (40%)
  blocking collectives  164 us (36%)
  matrix products  38.8 us (9%)
  local copies, waits for them, and re-layouts  35.3 us (8%)
  between operations  14.3 us (3%)
  other arithmetic  10.9 us (2%)
  starting transfers between devices  6.37 us (1%)
    unnamed x7, waiting for transfers between devices  132 us
    all_to_all x3, blocking collectives, fourier_spectrum(): lax.all_to_all(local_spectra, 'freq', split_axis=2, concat_axis=0, tiled=...  124 us
    all_to_all x1, blocking collectives, to_time(): lax.all_to_all(summed, 'freq', split_axis=0, concat_axis=2, tiled=True)  40.8 us
    all_to_all x1, waiting for transfers between devices, to_time(): lax.all_to_all(summed, 'freq', split_axis=0, concat_axis=2, tiled=True)  31.5 us
    dot_general x12, matrix products, product(): jnp.einsum('key,ekn->ykn', left_operand, right_operand, preferred_element...  27.9 us
    unnamed x48, local copies, waits for them, and re-layouts  23.4 us
    reduce_scatter x1, waiting for transfers between devices, on_device(): lax.psum_scatter(partial_corr.astype(jnp.bfloat16), 'rcv', scatter_dimens...  14.8 us
  transfers between devices with their start and end apart: 5, of which 5 were waited for; matrix products, arithmetic and copies ran while one was open for 0% of the time, Pallas kernels for 0%

commit v1 on v0

v1 whole, which is shorter than its diff:
```python
import math

import jax
import jax.numpy as jnp
from jax import lax
from jax.sharding import PartitionSpec as P

CHUNKS = 2


def lookup_tables(samples, frequencies):
    sample = jnp.arange(samples, dtype=jnp.int32)
    spectral_bin_index = jnp.arange(frequencies, dtype=jnp.int32)
    phase_index = sample[:, None] * spectral_bin_index[None, :] % samples
    angles = 2.0 * math.pi / samples * phase_index.astype(jnp.float32)
    cosine = jnp.cos(angles)
    sine = jnp.sin(angles)
    forward = (jnp.stack([cosine, -sine], axis=1) / math.sqrt(samples)).astype(jnp.bfloat16)
    inverse = (jnp.stack([cosine.T, -sine.T], axis=0) * (2.0 / math.sqrt(samples))).astype(
        jnp.bfloat16
    )
    return (forward, inverse)


def spectrum_of(field, forward):
    local = jnp.einsum(
        "sqt,tcf->sfcq", field, forward, preferred_element_type=jnp.float32
    ).astype(jnp.bfloat16)
    return local.reshape(local.shape[0], local.shape[1], -1)


def to_frequencies(local):
    return lax.all_to_all(local, "freq", split_axis=1, concat_axis=0, tiled=True)


def partial_product(spectra, reflection, sign):
    half = spectra.shape[2] // 2
    real = spectra[:, :, :half]
    imag = spectra[:, :, half:]
    turned = jnp.concatenate([-imag, real] if sign > 0 else [imag, -real], axis=2)
    operand = jnp.stack([spectra, turned], axis=0)
    return jnp.einsum(
        "cfsr,csfn->rfn", reflection, operand, preferred_element_type=jnp.float32
    ).astype(jnp.bfloat16)


def sum_blocks(partial):
    return lax.psum_scatter(partial, "rcv", scatter_dimension=0, tiled=True)


def to_traces(summed):
    return lax.all_to_all(summed, "freq", split_axis=0, concat_axis=1, tiled=True)


def inverse_window(summed, onset, inverse):
    spectra = summed.reshape(summed.shape[0], summed.shape[1], 2, -1)
    traces = jnp.einsum("sfcq,cft->sqt", spectra, inverse, preferred_element_type=jnp.float32)
    sample = jnp.arange(traces.shape[2], dtype=jnp.int32)
    window = (sample[None, None, :] < onset[:, :, None]).astype(jnp.float32)
    return traces * window


def on_device(reflection, direct, onset):
    samples = direct.shape[2]
    frequencies = reflection.shape[1] * lax.axis_size("freq")
    receivers = reflection.shape[3]
    forward, inverse = lookup_tables(samples, frequencies)
    width = direct.shape[1] // CHUNKS
    plus_out, minus_out, green_out = [], [], []
    for chunk in range(CHUNKS):
        part = slice(chunk * width, (chunk + 1) * width)
        field, edge = direct[:, part], onset[:, part]
        spectra = to_frequencies(spectrum_of(field, forward))
        back = to_traces(sum_blocks(partial_product(spectra, reflection, 1)))
        minus = inverse_window(back, edge, inverse).astype(jnp.bfloat16)
        minus_spectrum = to_frequencies(spectrum_of(minus, forward))
        back = to_traces(sum_blocks(partial_product(minus_spectrum, reflection, -1)))
        plus = (field.astype(jnp.float32) + inverse_window(back, edge, inverse)).astype(
            jnp.bfloat16
        )
        spectra = to_frequencies(spectrum_of(plus, forward))
        summed = sum_blocks(partial_product(spectra, reflection, 1)).astype(jnp.float32)
        green = (summed - minus_spectrum.astype(jnp.float32)).astype(jnp.bfloat16)
        plus_out.append(plus)
        minus_out.append(minus)
        green_out.append(green.reshape(green.shape[0], green.shape[1], 2, width))
    green = jnp.concatenate(green_out, axis=3)
    green_real = green[:, :, 0]
    green_imag = green[:, :, 1]

    def pairwise(left_operand, right_operand):
        return jnp.einsum(
            "rfa,rfb->fab", left_operand, right_operand, preferred_element_type=jnp.float32
        )

    real_part = pairwise(green_real, green_real) + pairwise(green_imag, green_imag)
    imag_part = pairwise(green_real, green_imag) - pairwise(green_imag, green_real)
    partial_corr = jnp.stack([real_part, imag_part], axis=0) / receivers
    correlation = lax.psum_scatter(
        partial_corr.astype(jnp.bfloat16), "rcv", scatter_dimension=2, tiled=True
    ).astype(jnp.float32)
    return (
        jnp.concatenate(plus_out, axis=1),
        jnp.concatenate(minus_out, axis=1),
        correlation,
    )


def solution(mesh):
    placed = (
        P(None, "freq", "rcv", None),
        P(("rcv", "freq"), None, None),
        P(("rcv", "freq"), None),
    )
    return jax.shard_map(
        on_device,
        mesh=mesh,
        in_specs=placed,
        out_specs=(
            P(("rcv", "freq"), None, None),
            P(("rcv", "freq"), None, None),
            P(None, "freq", "rcv", None),
        ),
        check_vma=False,
    )
```

time: 452 us -> 456 us (level)
  the two profiles are of different devices: /device:TPU:28 before, /device:TPU:0 now
where the time goes in v1:
time: 456 us; the launch traced here: 447 us
  local copies, waits for them, and re-layouts  118 us (26%)
  blocking collectives  102 us (22%)
  waiting for transfers between devices  100 us (22%)
  matrix products  54.7 us (12%)
  starting transfers between devices  31.1 us (7%)
  other arithmetic  25.8 us (6%)
  between operations  15.1 us (3%)
    all_to_all x4, blocking collectives, to_frequencies(): lax.all_to_all(local, 'freq', split_axis=1, concat_axis=0, tiled=True)  102 us
    unnamed x60, local copies, waits for them, and re-layouts  51.6 us
    unnamed x13, waiting for transfers between devices  48.8 us
    dot_general x6, matrix products, partial_product(): jnp.einsum('cfsr,csfn->rfn', reflection, operand, preferred_element_type=...  36.1 us
    all_to_all x2, waiting for transfers between devices, to_frequencies(): lax.all_to_all(local, 'freq', split_axis=1, concat_axis=0, tiled=True)  26 us
    all_to_all x4, starting transfers between devices, to_traces(): lax.all_to_all(summed, 'freq', split_axis=0, concat_axis=1, tiled=True)  19.8 us
    all_to_all x4, waiting for transfers between devices, to_traces(): lax.all_to_all(summed, 'freq', split_axis=0, concat_axis=1, tiled=True)  15.9 us
    reshape x4, local copies, waits for them, and re-layouts, inverse_window(): spectra = summed.reshape(summed.shape[0], summed.shape[1], 2, -1)  13.3 us
  transfers between devices with their start and end apart: 13, of which 8 were waited for; matrix products, arithmetic and copies ran while one was open for 28% of the time, Pallas kernels for 0%

profile of v1, /device:TPU:0, one launch (start us, length us, event | category | flops | bytes accessed | tf_op | source)
XLA Modules:
  0.0 447.1 jit_solution(15853837104393237194)
XLA Ops:
  10.8 27.3 %all_to_all.168 = bf16[24,128,128]{2,0,1:T(8,128)(2,1)S(1)} all-to-all(bf16[24,128,128]{2,0,1:T(8,128)(2,1)S(1)} %copy.163), channel_id=1, replica_groups=mesh['freq'=16,'rcv'=2] {'freq'}, dimensions={1} | all-to-all | bytes 1572864 | tf_op jit(solution)/shard_map/all_to_all | solution.py:33
  40.4 5.3 %bitcast_convert_fusion.5 = bf16[8,128,768]{2,1,0:T(8,128)(2,1)S(1)} fusion(bf16[2,8,384,768]{3,2,1,0:T(8,128)(2,1)} %param.3, bf16[1,384,8,128]{1,3,0,2:T(8,128)(2,1)S(1)} %maximum_bitcast_fusion, bf16[1,384,8,128]{1,3,0,2:T(8,128)(2,1)S(1)} %copy.169), kind=kOutput, calls=%fused_computation.29 | convolution fusion | flops 1209532416 | bytes 12582912 | tf_op jit(solution)/shard_map/cfsr,csfn->rfn/dot_general | solution.py:42
  49.8 24.3 %all_to_all.169 = bf16[24,128,128]{2,0,1:T(8,128)(2,1)S(1)} all-to-all(bf16[24,128,128]{2,0,1:T(8,128)(2,1)S(1)} %copy.187), channel_id=1, replica_groups=mesh['freq'=16,'rcv'=2] {'freq'}, dimensions={1} | all-to-all | bytes 1572864 | tf_op jit(solution)/shard_map/all_to_all | solution.py:33
  76.4 5.3 %bitcast_convert_fusion.3 = bf16[8,128,768]{2,1,0:T(8,128)(2,1)S(1)} fusion(bf16[2,8,384,768]{3,2,1,0:T(8,128)(2,1)} %param.3, bf16[1,384,8,128]{1,3,0,2:T(8,128)(2,1)S(1)} %maximum_bitcast_fusion.2, bf16[1,384,8,128]{1,3,0,2:T(8,128)(2,1)S(1)} %copy.193), kind=kOutput, calls=%fused_computation.22 | convolution fusion | flops 1209532416 | bytes 12582912 | tf_op jit(solution)/shard_map/cfsr,csfn->rfn/dot_general | solution.py:42
  86.2 3.9 all-to-all-start.1
  90.1 18.8 %reduce-scatter.26.cloned.1.call-done = bf16[384,1024]{1,0:T(8,128)(2,1)} async-done(((bf16[768,1024]{1,0:T(8,128)(2,1)}), bf16[384,1024]{1,0:T(8,128)(2,1)}) %reduce-scatter.26.cloned.1.call-update) | async-done | bytes 786448
  111.7 5.8 %all-to-all-start.5 = ((bf16[384,8,128]{2,1,0:T(8,128)(2,1)}), bf16[384,8,128]{2,1,0:T(8,128)(2,1)S(1)}, u32[]{:S(2)}, u32[]{:S(2)}) async-start(bf16[384,8,128]{2,1,0:T(8,128)(2,1)} %copy.195), calls=%async_computation.5 | async-start | bytes 1572864 | tf_op jit(solution)/shard_map/all_to_all | solution.py:52
  125.4 10.8 %all-to-all-done.5 = bf16[384,8,128]{2,1,0:T(8,128)(2,1)S(1)} async-done(((bf16[384,8,128]{2,1,0:T(8,128)(2,1)}), bf16[384,8,128]{2,1,0:T(8,128)(2,1)S(1)}, u32[]{:S(2)}, u32[]{:S(2)}) %all-to-all-start.5) | async-done | bytes 786464 | tf_op jit(solution)/shard_map/all_to_all | solution.py:52
  136.2 5.4 %all-to-all-start.2 = ((bf16[24,128,128]{2,0,1:T(8,128)(2,1)}), bf16[24,128,128]{2,0,1:T(8,128)(2,1)S(1)}, u32[]{:S(2)}, u32[]{:S(2)}) async-start(bf16[24,128,128]{2,0,1:T(8,128)(2,1)} %copy.175), calls=%async_computation.2 | async-start | bytes 1572864 | tf_op jit(solution)/shard_map/all_to_all | solution.py:33
  142.9 3.9 reshape.199
  146.8 13.5 %all-to-all-done.2 = bf16[24,128,128]{2,0,1:T(8,128)(2,1)S(1)} async-done(((bf16[24,128,128]{2,0,1:T(8,128)(2,1)}), bf16[24,128,128]{2,0,1:T(8,128)(2,1)S(1)}, u32[]{:S(2)}, u32[]{:S(2)}) %all-to-all-start.2) | async-done | bytes 786464 | tf_op jit(solution)/shard_map/all_to_all | solution.py:33
  169.4 6.4 %bitcast_convert_fusion.4 = bf16[8,128,768]{2,1,0:T(8,128)(2,1)} fusion(bf16[2,8,384,768]{3,2,1,0:T(8,128)(2,1)} %param.3, bf16[1,384,8,128]{1,3,0,2:T(8,128)(2,1)S(1)} %maximum_bitcast_fusion.1, bf16[1,384,8,128]{1,3,0,2:T(8,128)(2,1)S(1)} %copy-done.13), kind=kOutput, calls=%fused_computation.26 | convolution fusion | flops 1209532416 | bytes 12582912 | tf_op jit(solution)/shard_map/cfsr,csfn->rfn/dot_general | solution.py:42
  175.8 2.6 copy.279
  185.5 25.2 %all_to_all.170 = bf16[24,128,128]{2,0,1:T(8,128)(2,1)S(1)} all-to-all(bf16[24,128,128]{2,0,1:T(8,128)(2,1)S(1)} %copy.199), channel_id=1, replica_groups=mesh['freq'=16,'rcv'=2] {'freq'}, dimensions={1} | all-to-all | bytes 1572864 | tf_op jit(solution)/shard_map/all_to_all | solution.py:33
  221.4 6.4 %bitcast_convert_fusion.2 = bf16[8,128,768]{2,1,0:T(8,128)(2,1)} fusion(bf16[2,8,384,768]{3,2,1,0:T(8,128)(2,1)} %param.3, bf16[1,384,8,128]{1,3,0,2:T(8,128)(2,1)S(1)} %maximum_bitcast_fusion.3, bf16[1,384,8,128]{1,3,0,2:T(8,128)(2,1)S(1)} %copy-done.14), kind=kOutput, calls=%fused_computation.19 | convolution fusion | flops 1209532416 | bytes 12582912 | tf_op jit(solution)/shard_map/cfsr,csfn->rfn/dot_general | solution.py:42
  235.2 4.5 %all-to-all-start.3 = ((bf16[384,8,128]{2,1,0:T(8,128)(2,1)}), bf16[384,8,128]{2,1,0:T(8,128)(2,1)}, u32[]{:S(2)}, u32[]{:S(2)}) async-start(bf16[384,8,128]{2,1,0:T(8,128)(2,1)} %copy.183), calls=%async_computation.3 | async-start | bytes 1572864 | tf_op jit(solution)/shard_map/all_to_all | solution.py:52
  239.7 15.4 %reduce-scatter.28.cloned.1.call-done = bf16[384,1024]{1,0:T(8,128)(2,1)} async-done(((bf16[768,1024]{1,0:T(8,128)(2,1)}), bf16[384,1024]{1,0:T(8,128)(2,1)}) %reduce-scatter.28.cloned.1.call-update) | async-done | bytes 786448
  259.9 5.7 %all-to-all-start.7 = ((bf16[384,8,128]{2,1,0:T(8,128)(2,1)}), bf16[384,8,128]{2,1,0:T(8,128)(2,1)}, u32[]{:S(2)}, u32[]{:S(2)}) async-start(bf16[384,8,128]{2,1,0:T(8,128)(2,1)} %copy.207), calls=%async_computation.7 | async-start | bytes 1572864 | tf_op jit(solution)/shard_map/all_to_all | solution.py:52
  267.8 3.9 reshape.197
  271.7 3.0 fusion.16
  279.2 5.1 %all-to-all-done.7 = bf16[384,8,128]{2,1,0:T(8,128)(2,1)} async-done(((bf16[384,8,128]{2,1,0:T(8,128)(2,1)}), bf16[384,8,128]{2,1,0:T(8,128)(2,1)}, u32[]{:S(2)}, u32[]{:S(2)}) %all-to-all-start.7) | async-done | bytes 786464 | tf_op jit(solution)/shard_map/all_to_all | solution.py:52
  284.3 5.4 %all-to-all-start.8 = ((bf16[24,128,128]{2,0,1:T(8,128)(2,1)}), bf16[24,128,128]{2,0,1:T(8,128)(2,1)}, u32[]{:S(2)}, u32[]{:S(2)}) async-start(bf16[24,128,128]{2,0,1:T(8,128)(2,1)} %copy.211), calls=%async_computation.8 | async-start | bytes 1572864 | tf_op jit(solution)/shard_map/all_to_all | solution.py:33
  292.0 3.9 reshape.201
  295.9 12.6 %all-to-all-done.8 = bf16[24,128,128]{2,0,1:T(8,128)(2,1)} async-done(((bf16[24,128,128]{2,0,1:T(8,128)(2,1)}), bf16[24,128,128]{2,0,1:T(8,128)(2,1)}, u32[]{:S(2)}, u32[]{:S(2)}) %all-to-all-start.8) | async-done | bytes 786464 | tf_op jit(solution)/shard_map/all_to_all | solution.py:33
  322.2 6.4 %bitcast_convert_fusion.1 = bf16[8,128,768]{2,1,0:T(8,128)(2,1)} fusion(bf16[2,8,384,768]{3,2,1,0:T(8,128)(2,1)} %param.3, bf16[1,384,8,128]{1,3,0,2:T(8,128)(2,1)S(1)} %maximum_bitcast_fusion.4, bf16[1,384,8,128]{1,3,0,2:T(8,128)(2,1)S(1)} %copy-done.11), kind=kOutput, calls=%fused_computation.15 | convolution fusion | flops 1209532416 | bytes 12582912 | tf_op jit(solution)/shard_map/cfsr,csfn->rfn/dot_general | solution.py:42
  331.2 3.0 fusion.13
  336.3 2.6 copy.222
  339.0 25.6 %all_to_all.171 = bf16[24,128,128]{2,0,1:T(8,128)(2,1)S(1)} all-to-all(bf16[24,128,128]{2,0,1:T(8,128)(2,1)} %copy.222), channel_id=1, replica_groups=mesh['freq'=16,'rcv'=2] {'freq'}, dimensions={1} | all-to-all | bytes 1572864 | tf_op jit(solution)/shard_map/all_to_all | solution.py:33
  376.4 6.4 %bitcast_convert_fusion = bf16[8,128,768]{2,1,0:T(8,128)(2,1)} fusion(bf16[2,8,384,768]{3,2,1,0:T(8,128)(2,1)} %param.3, bf16[1,384,8,128]{1,3,0,2:T(8,128)(2,1)S(1)} %maximum_bitcast_fusion.5, bf16[1,384,8,128]{1,3,0,2:T(8,128)(2,1)S(1)} %copy-done.12), kind=kOutput, calls=%fused_computation.14 | convolution fusion | flops 1209532416 | bytes 12582912 | tf_op jit(solution)/shard_map/cfsr,csfn->rfn/dot_general | solution.py:42
  382.8 2.6 copy.287
  395.6 14.5 %reduce-scatter.32.cloned.1.call-done = bf16[384,1024]{1,0:T(8,128)(2,1)} async-done(((bf16[768,1024]{1,0:T(8,128)(2,1)}), bf16[384,1024]{1,0:T(8,128)(2,1)}) %reduce-scatter.32.cloned.1.call-update) | async-done | bytes 786448
  428.7 9.3 %reduce-scatter.20.cloned.1.call-done = bf16[2,8,64,128]{3,2,1,0:T(8,128)(2,1)} async-done(((bf16[2,8,128,128]{3,2,1,0:T(8,128)(2,1)}), bf16[2,8,64,128]{3,2,1,0:T(8,128)(2,1)}) %reduce-scatter.20.cloned.1.call-update) | async-done | bytes 262160 | tf_op jit(solution)/shard_map/reduce_scatter | solution.py:99
  (157 shorter events, 137.4 us)
Async XLA Ops:
  7.2 76.1 %reduce-scatter.22.cloned.1.call-start = ((), (), s32[]{:S(2)}) async-start(), calls=%async_computation.18 | async-start | bytes 2359296
  47.3 61.6 %reduce-scatter.26.cloned.1.call-start = ((), (), s32[]{:S(2)}) async-start(), calls=%async_computation.20 | async-start | bytes 2359296
  86.2 25.6 %all-to-all-start.1 = ((bf16[384,8,128]{2,1,0:T(8,128)(2,1)}), bf16[384,8,128]{2,1,0:T(8,128)(2,1)S(1)}, u32[]{:S(2)}, u32[]{:S(2)}) async-start(bf16[384,8,128]{2,1,0:T(8,128)(2,1)} %copy.171), calls=%async_computation.1 | async-start | bytes 1572864 | tf_op jit(solution)/shard_map/all_to_all | solution.py:52
  111.7 7.6 %copy-start.17 = (s32[24,128]{1,0:T(8,128)S(1)}, s32[24,128]{1,0:T(8,128)}, u32[]{:S(2)}) copy-start(s32[24,128]{1,0:T(8,128)} %param.5) | copy-start | bytes 36868
  111.7 24.4 %all-to-all-start.5 = ((bf16[384,8,128]{2,1,0:T(8,128)(2,1)}), bf16[384,8,128]{2,1,0:T(8,128)(2,1)S(1)}, u32[]{:S(2)}, u32[]{:S(2)}) async-start(bf16[384,8,128]{2,1,0:T(8,128)(2,1)} %copy.195), calls=%async_computation.5 | async-start | bytes 1572864 | tf_op jit(solution)/shard_map/all_to_all | solution.py:52
  119.6 1.6 copy-start.15
  136.2 24.1 %all-to-all-start.2 = ((bf16[24,128,128]{2,0,1:T(8,128)(2,1)}), bf16[24,128,128]{2,0,1:T(8,128)(2,1)S(1)}, u32[]{:S(2)}, u32[]{:S(2)}) async-start(bf16[24,128,128]{2,0,1:T(8,128)(2,1)} %copy.175), calls=%async_computation.2 | async-start | bytes 1572864 | tf_op jit(solution)/shard_map/all_to_all | solution.py:33
  141.6 88.9 %reduce-scatter.24.cloned.1.call-start = ((), (), s32[]{:S(2)}) async-start(), calls=%async_computation.19 | async-start | bytes 2359296
  166.9 1.4 copy-start.9
  166.9 1.4 copy-start.10
  168.3 1.1 copy-start.13
  178.4 0.9 copy-start.16
  178.4 76.7 %reduce-scatter.28.cloned.1.call-start = ((), (), s32[]{:S(2)}) async-start(), calls=%async_computation.21 | async-start | bytes 2359296
  181.6 1.2 copy-start
  220.1 1.4 copy-start.14
  235.2 24.6 %all-to-all-start.3 = ((bf16[384,8,128]{2,1,0:T(8,128)(2,1)}), bf16[384,8,128]{2,1,0:T(8,128)(2,1)}, u32[]{:S(2)}, u32[]{:S(2)}) async-start(bf16[384,8,128]{2,1,0:T(8,128)(2,1)} %copy.183), calls=%async_computation.3 | async-start | bytes 1572864 | tf_op jit(solution)/shard_map/all_to_all | solution.py:52
  259.9 24.4 %all-to-all-start.7 = ((bf16[384,8,128]{2,1,0:T(8,128)(2,1)}), bf16[384,8,128]{2,1,0:T(8,128)(2,1)}, u32[]{:S(2)}, u32[]{:S(2)}) async-start(bf16[384,8,128]{2,1,0:T(8,128)(2,1)} %copy.207), calls=%async_computation.7 | async-start | bytes 1572864 | tf_op jit(solution)/shard_map/all_to_all | solution.py:52
  274.7 1.1 copy-start.2
  284.3 24.2 %all-to-all-start.8 = ((bf16[24,128,128]{2,0,1:T(8,128)(2,1)}), bf16[24,128,128]{2,0,1:T(8,128)(2,1)}, u32[]{:S(2)}, u32[]{:S(2)}) async-start(bf16[24,128,128]{2,0,1:T(8,128)(2,1)} %copy.211), calls=%async_computation.8 | async-start | bytes 1572864 | tf_op jit(solution)/shard_map/all_to_all | solution.py:33
  289.7 95.8 %reduce-scatter.30.cloned.1.call-start = ((), (), s32[]{:S(2)}) async-start(), calls=%async_computation.22 | async-start | bytes 2359296
  309.7 0.9 copy-start.6
  320.8 1.4 copy-start.11
  331.2 78.9 %reduce-scatter.32.cloned.1.call-start = ((), (), s32[]{:S(2)}) async-start(), calls=%async_computation.23 | async-start | bytes 2359296
  334.3 1.1 copy-start.4
  364.7 0.9 copy-start.7
  375.1 1.3 copy-start.12
  385.4 52.6 %reduce-scatter.20.cloned.1.call-start = ((), (), s32[]{:S(2)}) async-start(), calls=%async_computation.17 | async-start | bytes 786432 | tf_op jit(solution)/shard_map/reduce_scatter | solution.py:99
  415.7 2.6 copy-start.8
  422.2 1.6 copy-start.1
  423.8 1.9 copy-start.3
  423.8 3.0 copy-start.5
Sparse Core Ops, SparseCore 0:
  47.4 25.4 reduce-scatter.21
  83.4 25.4 reduce-scatter.25
  178.5 25.9 reduce-scatter.23
  230.6 24.5 reduce-scatter.27
  331.3 25.9 reduce-scatter.29
  385.6 24.4 reduce-scatter.31
  423.3 14.6 reduce-scatter.19

commit v2 on v0

--- a/solution.py
+++ b/solution.py
@@ -1,8 +1,11 @@
+import functools
 import math
 
 import jax
 import jax.numpy as jnp
 from jax import lax
+from jax.experimental import pallas as pl
+from jax.experimental.pallas import tpu as pltpu
 from jax.sharding import PartitionSpec as P
 
 
@@ -101,6 +104,369 @@
     return (focus_plus, focus_minus, correlation)
 
 
+CHUNKS = 2
+GROUP = 4
+MESH = pl.DeviceIdType.MESH
+
+
+def kernel(
+    n, direct, onset, fwd, inv, refl, fp, fm, corr,
+    ref_t, stage, zs, zr, ys, yr, rs, rr, own, minus, green, rows, cs, cr,
+    load_sem, z_send, z_recv, y_send, y_recv, r_send, r_recv, c_send, c_recv,
+):
+    me = lax.axis_index("freq")
+    side = lax.axis_index("rcv")
+    other = 1 - side
+    traces, points, samples = direct.shape
+    width = points // CHUNKS
+    lanes = 2 * width
+    bins, receivers, _ = ref_t.shape
+    sources = receivers // 2
+    freqs = n * bins
+    groups = traces // GROUP
+    f32, bf16 = jnp.float32, jnp.bfloat16
+
+    barrier = pltpu.get_barrier_semaphore()
+
+    def greet(k, carry):
+        pl.semaphore_signal(
+            barrier, inc=1, device_id=(lax.rem(me + k, n), side), device_id_type=MESH
+        )
+        return carry
+
+    lax.fori_loop(1, n, greet, 0)
+    pl.semaphore_signal(barrier, inc=1, device_id=(me, other), device_id_type=MESH)
+
+    def load(f):
+        slot = lax.rem(f, 2)
+        return pltpu.make_async_copy(refl.at[:, f], stage.at[slot], load_sem.at[slot])
+
+    load(0).start()
+    load(1).start()
+
+    def exchange(src, dst, send, recv, k):
+        o = n // 2 + k
+        off = o - (n - 1) * (o // n)
+        peer = lax.rem(me + off, n)
+        return pltpu.make_async_remote_copy(
+            src_ref=src.at[peer],
+            dst_ref=dst.at[me],
+            send_sem=send.at[off],
+            recv_sem=recv.at[off],
+            device_id=(peer, side),
+            device_id_type=MESH,
+        )
+
+    def arrival(src, dst, send, recv, off):
+        giver = lax.rem(me - off + n, n)
+        return pltpu.make_async_remote_copy(
+            src_ref=src.at[giver],
+            dst_ref=dst.at[giver],
+            send_sem=send.at[off],
+            recv_sem=recv.at[off],
+            device_id=(giver, side),
+            device_id_type=MESH,
+        )
+
+    def send_all(ops):
+        def step(k, carry):
+            exchange(*ops, k).start()
+            return carry
+
+        lax.fori_loop(0, n - 1, step, 0)
+        src, dst = ops[0], ops[1]
+        dst[me] = src[me]
+
+    def wait_all(ops):
+        def step(off, carry):
+            arrival(*ops, off).wait_recv()
+            return carry
+
+        lax.fori_loop(1, n, step, 0)
+
+    def drain_all(ops):
+        def step(off, carry):
+            arrival(*ops, off).wait_send()
+            return carry
+
+        lax.fori_loop(1, n, step, 0)
+
+    def z_ops(p, c):
+        return zs.at[p, c], zr.at[p, c], z_send.at[p, c], z_recv.at[p, c]
+
+    def y_ops(p, c):
+        return ys.at[p, c], yr.at[p, c], y_send.at[p, c], y_recv.at[p, c]
+
+    def half_copy(p, c, f):
+        return pltpu.make_async_remote_copy(
+            src_ref=rs.at[p, c, f],
+            dst_ref=rr.at[p, c, f],
+            send_sem=r_send.at[p, c, f],
+            recv_sem=r_recv.at[p, c, f],
+            device_id=(me, other),
+            device_id_type=MESH,
+        )
+
+    def corr_copy(f):
+        return pltpu.make_async_remote_copy(
+            src_ref=cs.at[other, f],
+            dst_ref=cr.at[f],
+            send_sem=c_send.at[f],
+            recv_sem=c_recv.at[f],
+            device_id=(me, other),
+            device_id_type=MESH,
+        )
+
+    def to_spectrum(p, c, g, block):
+        spec = jnp.dot(block, fwd[...], preferred_element_type=f32)
+        for u in range(GROUP):
+            a = spec[u * width : (u + 1) * width]
+            turned = jnp.concatenate([a[:, :freqs], a[:, freqs:]], axis=0).T
+            zs[p, c, :, g * GROUP + u] = turned.reshape(n, bins, lanes).astype(bf16)
+
+    def first(c):
+        def step(g, carry):
+            block = direct[pl.ds(g * GROUP, GROUP), c * width : (c + 1) * width, :]
+            to_spectrum(0, c, g, block.reshape(GROUP * width, samples))
+            return carry
+
+        lax.fori_loop(0, groups, step, 0)
+
+    def unpack(src):
+        size = traces * bins
+
+        def step(j, carry):
+            rows[pl.ds(pl.multiple_of(j * size, size), size), :] = (
+                src[j].astype(f32).reshape(size, lanes)
+            )
+            return carry
+
+        lax.fori_loop(0, n, step, 0)
+
+    def back(p, c):
+        wait_all(y_ops(p, c))
+        unpack(yr.at[p, c])
+        cols = slice(c * width, (c + 1) * width)
+
+        def step(g, carry):
+            parts = []
+            for u in range(GROUP):
+                t = rows[pl.ds(g * GROUP + u, freqs, stride=traces), :].T
+                parts.append(jnp.concatenate([t[:width], t[width:]], axis=1))
+            lhs = jnp.concatenate(parts, axis=0).astype(bf16)
+            out = jnp.dot(lhs, inv[...], preferred_element_type=f32)
+            size = GROUP * width
+            edge = onset[c, pl.ds(pl.multiple_of(g * size, size), size), :]
+            sample = lax.broadcasted_iota(jnp.int32, out.shape, 1)
+            out = jnp.where(sample < edge, out, 0.0)
+            at = pl.ds(g * GROUP, GROUP)
+            if p == 0:
+                block = out.astype(bf16)
+                fm[at, cols, :] = block.reshape(GROUP, width, samples)
+            else:
+                old = direct[at, cols, :].astype(f32).reshape(size, samples)
+                block = (old + out).astype(bf16)
+                fp[at, cols, :] = block.reshape(GROUP, width, samples)
+            to_spectrum(p + 1, c, g, block)
+            return carry
+
+        lax.fori_loop(0, groups, step, 0)
+        send_all(z_ops(p + 1, c))
+
+    def apply(p, c, sign):
+        wait_all(z_ops(p, c))
+        unpack(zr.at[p, c])
+
+        def step(f, carry):
+            x = rows[pl.ds(f, sources, stride=bins), :]
+            if p == 1:
+                minus[c, f] = x.astype(bf16)
+            y = pltpu.roll(x, width, 1)
+            low = lax.broadcasted_iota(jnp.int32, x.shape, 1) < width
+            y = jnp.where(low, -y, y) if sign > 0 else jnp.where(low, y, -y)
+            w = jnp.concatenate([x.astype(bf16), y.astype(bf16)], axis=0)
+            theirs = ref_t[f, pl.ds(pl.multiple_of(other * sources, sources), sources), :]
+            rs[p, c, f] = jnp.dot(theirs, w, preferred_element_type=f32).astype(bf16)
+            half_copy(p, c, f).start()
+            mine = ref_t[f, pl.ds(pl.multiple_of(side * sources, sources), sources), :]
+            own[c, f] = jnp.dot(mine, w, preferred_element_type=f32).astype(bf16)
+            return carry
+
+        lax.fori_loop(0, bins, step, 0)
+
+    def reduce(p, c):
+        def step(f, carry):
+            half_copy(p, c, f).wait_recv()
+            total = own[c, f].astype(f32) + rr[p, c, f].astype(f32)
+            if p < 2:
+                ys[p, c, :, f] = total.reshape(n, traces, lanes).astype(bf16)
+            else:
+                green[c, f] = (total - minus[c, f].astype(f32)).astype(bf16)
+            return carry
+
+        lax.fori_loop(0, bins, step, 0)
+        if p < 2:
+            send_all(y_ops(p, c))
+
+    def transpose(f, carry):
+        load(f).wait()
+        slot = lax.rem(f, 2)
+        for c in range(2):
+            ref_t[f, :, c * sources : (c + 1) * sources] = stage[slot, c].T
+
+        @pl.when(f + 2 < bins)
+        def _():
+            load(f + 2).start()
+
+        return carry
+
+    first(0)
+    pl.semaphore_wait(barrier, n)
+    send_all(z_ops(0, 0))
+    first(1)
+    send_all(z_ops(0, 1))
+    lax.fori_loop(0, bins, transpose, 0)
+    apply(0, 0, 1)
+    reduce(0, 0)
+    apply(0, 1, 1)
+    reduce(0, 1)
+    back(0, 0)
+    back(0, 1)
+    apply(1, 0, -1)
+    reduce(1, 0)
+    apply(1, 1, -1)
+    reduce(1, 1)
+    back(1, 0)
+    back(1, 1)
+    apply(2, 0, 1)
+    reduce(2, 0)
+    apply(2, 1, 1)
+    reduce(2, 1)
+
+    half = points // 2
+
+    def correlate(f, carry):
+        a, b = green[0, f].astype(f32), green[1, f].astype(f32)
+        low = lax.broadcasted_iota(jnp.int32, a.shape, 1) < width
+        real = jnp.where(low, a, pltpu.roll(b, width, 1))
+        imag = jnp.where(low, pltpu.roll(a, width, 1), b)
+        both = jnp.concatenate([real, imag], axis=1).astype(bf16)
+        prod = lax.dot_general(
+            both, both, (((0,), (0,)), ((), ())), preferred_element_type=f32
+        )
+        re = (prod[:points, :points] + prod[points:, points:]) / receivers
+        im = (prod[:points, points:] - prod[points:, :points]) / receivers
+        for h in range(2):
+            cs[h, f, 0] = re[h * half : (h + 1) * half].astype(bf16)
+            cs[h, f, 1] = im[h * half : (h + 1) * half].astype(bf16)
+        corr_copy(f).start()
+        return carry
+
+    lax.fori_loop(0, bins, correlate, 0)
+
+    def collect(f, carry):
+        corr_copy(f).wait_recv()
+        for c in range(2):
+            corr[c, f] = cs[side, f, c].astype(f32) + cr[f, c].astype(f32)
+        return carry
+
+    lax.fori_loop(0, bins, collect, 0)
+
+    for c in range(CHUNKS):
+        for p in range(3):
+            drain_all(z_ops(p, c))
+
+            def drain(f, carry):
+                half_copy(p, c, f).wait_send()
+                return carry
+
+            lax.fori_loop(0, bins, drain, 0)
+        for p in range(2):
+            drain_all(y_ops(p, c))
+
+    def drain_corr(f, carry):
+        corr_copy(f).wait_send()
+        return carry
+
+    lax.fori_loop(0, bins, drain_corr, 0)
+
+
+def fused(reflection, direct, onset):
+    n = lax.axis_size("freq")
+    traces, points, samples = direct.shape
+    _, bins, sources, receivers = reflection.shape
+    width = points // CHUNKS
+    frequencies = bins * n
+    forward, inverse = lookup_tables(samples, frequencies)
+    forward = forward.reshape(samples, 2 * frequencies)
+    inverse = inverse.reshape(2 * frequencies, samples)
+    edges = onset.reshape(traces, CHUNKS, width).transpose(1, 0, 2)
+    edges = edges.reshape(CHUNKS, traces * width, 1)
+    bf16, dma = jnp.bfloat16, pltpu.SemaphoreType.DMA
+    lanes = 2 * width
+    vmem = pl.BlockSpec(memory_space=pltpu.VMEM)
+    return pl.pallas_call(
+        functools.partial(kernel, n),
+        out_shape=(
+            jax.ShapeDtypeStruct(direct.shape, bf16),
+            jax.ShapeDtypeStruct(direct.shape, bf16),
+            jax.ShapeDtypeStruct((2, bins, points // 2, points), jnp.float32),
+        ),
+        in_specs=[vmem, vmem, vmem, vmem, pl.BlockSpec(memory_space=pl.ANY)],
+        out_specs=(vmem, vmem, vmem),
+        scratch_shapes=[
+            pltpu.VMEM((bins, receivers, 2 * sources), bf16),
+            pltpu.VMEM((2, 2, sources, receivers), bf16),
+            pltpu.VMEM((3, CHUNKS, n, traces, bins, lanes), bf16),
+            pltpu.VMEM((3, CHUNKS, n, traces, bins, lanes), bf16),
+            pltpu.VMEM((2, CHUNKS, n, bins, traces, lanes), bf16),
+            pltpu.VMEM((2, CHUNKS, n, bins, traces, lanes), bf16),
+            pltpu.VMEM((3, CHUNKS, bins, sources, lanes), bf16),
+            pltpu.VMEM((3, CHUNKS, bins, sources, lanes), bf16),
+            pltpu.VMEM((CHUNKS, bins, sources, lanes), bf16),
+            pltpu.VMEM((CHUNKS, bins, sources, lanes), bf16),
+            pltpu.VMEM((CHUNKS, bins, sources, lanes), bf16),
+            pltpu.VMEM((n * traces * bins, lanes), jnp.float32),
+            pltpu.VMEM((2, bins, 2, points // 2, points), bf16),
+            pltpu.VMEM((bins, 2, points // 2, points), bf16),
+            dma((2,)),
+            dma((3, CHUNKS, n)),
+            dma((3, CHUNKS, n)),
+            dma((2, CHUNKS, n)),
+            dma((2, CHUNKS, n)),
+            dma((3, CHUNKS, bins)),
+            dma((3, CHUNKS, bins)),
+            dma((bins,)),
+            dma((bins,)),
+        ],
+        compiler_params=pltpu.CompilerParams(
+            collective_id=0, has_side_effects=True, vmem_limit_bytes=67043328
+        ),
+    )(direct, edges, forward, inverse, reflection)
+
+
+def fits(reflection, direct):
+    n = lax.axis_size("freq")
+    traces, points, samples = direct.shape
+    _, bins, sources, receivers = reflection.shape
+    return (
+        lax.axis_size("rcv") == 2
+        and receivers == 2 * sources
+        and sources == n * traces
+        and traces % 8 == 0
+        and bins % 8 == 0
+        and points == 128
+        and samples % 128 == 0
+        and (bins * n) % 128 == 0
+    )
+
+
+def per_device(reflection, direct, onset):
+    if fits(reflection, direct):
+        return fused(reflection, direct, onset)
+    return on_device(reflection, direct, onset)
+
+
 def solution(mesh):
     placed = (
         P(None, "freq", "rcv", None),
@@ -108,7 +474,7 @@
         P(("rcv", "freq"), None),
     )
     return jax.shard_map(
-        on_device,
+        per_device,
         mesh=mesh,
         in_specs=placed,
         out_specs=(

time: 452 us -> 259 us (0.57)
  Pallas kernels: 0 us -> 245 us
  waiting for transfers between devices: 179 us -> 0 us
  blocking collectives: 164 us -> 0 us
  matrix products: 38.8 us -> 0 us
  local copies, waits for them, and re-layouts: 35.3 us -> 9.96 us
  between operations: 14.3 us -> 0.67 us
  other arithmetic: 10.9 us -> 3.59 us
  starting transfers between devices: 6.37 us -> 0 us
    pallas_call x0 -> x1, Pallas kernels: none -> 245 us  [fused(): pl.pallas_call(functools.partial(kernel, n), out_shape=(jax.ShapeDtypeStr...]
    all_to_all x4 -> x0, blocking collectives: 164 us -> none  [the longest x3 124 us: fourier_spectrum(): lax.all_to_all(local_spectra, 'freq', split_axis=2, concat_axis=0, tiled=...]
    unnamed x7 -> x0, waiting for transfers between devices: 132 us -> none
    dot_general x21 -> x0, matrix products: 38.8 us -> none  [the longest x12 27.9 us: product(): jnp.einsum('key,ekn->ykn', left_operand, right_operand, preferred_element...]
    all_to_all x1 -> x0, waiting for transfers between devices: 31.5 us -> none  [to_time(): lax.all_to_all(summed, 'freq', split_axis=0, concat_axis=2, tiled=True)]
    unnamed x48 -> x7, local copies, waits for them, and re-layouts: 23.4 us -> 6.47 us
    reduce_scatter x1 -> x0, waiting for transfers between devices: 14.8 us -> none  [on_device(): lax.psum_scatter(partial_corr.astype(jnp.bfloat16), 'rcv', scatter_dimens...]
    all_to_all x1 -> x0, starting transfers between devices: 6.03 us -> none  [to_time(): lax.all_to_all(summed, 'freq', split_axis=0, concat_axis=2, tiled=True)]
  transfers between devices with their start and end apart: 5 -> 0, of which waited for: 5 -> 0; matrix products, arithmetic and copies ran while one was open for 0% -> 0% of each run, Pallas kernels for 0% -> 0%
where the time goes in v2:
time: 259 us
  Pallas kernels  245 us (95%)
  local copies, waits for them, and re-layouts  9.96 us (4%)
  other arithmetic  3.59 us (1%)
    pallas_call x1, Pallas kernels, fused(): pl.pallas_call(functools.partial(kernel, n), out_shape=(jax.ShapeDtypeStr...  245 us
    unnamed x7, local copies, waits for them, and re-layouts  6.47 us

profile of v2, /device:TPU:28, one launch (start us, length us, event | category | flops | bytes accessed | tf_op | source)
XLA Modules:
  0.0 259.1 jit_solution(15530083785271064342)
XLA Ops:
  0.6 0.8 reshape.162
  1.4 1.0 sine_negate_fusion.1
  2.5 0.8 copy_bitcast_fusion.fwd
  3.2 1.0 sine_negate_fusion
  4.3 0.7 fusion.1
  5.0 2.7 %reshape.164.onset = s32[2,1536,1]{2,1,0:T(8,128)} reshape(s32[2,24,64]{2,1,0:T(8,128)S(1)} %bitcast.10) | data formatting | bytes 24576 | tf_op jit(solution)/shard_map/reshape | solution.py:404
  7.7 244.9 %shard_map.58 = (bf16[24,128,512]{2,1,0:T(8,128)(2,1)}, bf16[24,128,512]{2,1,0:T(8,128)(2,1)}, f32[2,8,64,128]{3,2,1,0:T(8,128)}) custom-call(bf16[24,128,512]{2,1,0:T(8,128)(2,1)} %direct.1, s32[2,1536,1]{2,1,0:T(8,128)} %reshape.164.onset, bf16[512,256]{1,0:T(8,128)(2,1)} %copy_bitcast_fusion.fwd, bf16[256,512]{1,0:T(8,128)(2,1)} %bitcast.9, ...), custom_call_target="tpu_custom_call" | custom-call | tf_op jit(solution)/shard_map/pallas_call | solution.py:408
  252.6 0.0 copy-start
  252.7 4.0 %copy.19 = bf16[24,128,512]{2,1,0:T(8,128)(2,1)} copy(bf16[24,128,512]{2,1,0:T(8,128)(2,1)} %get-tuple-element.10) | data formatting | bytes 6291456
  256.7 0.0 copy-done
  256.7 0.0 copy-start.1
  256.7 1.7 copy.20
  258.3 0.0 copy-done.1
  258.3 0.8 copy.21
  (1 shorter events, 0.0 us)
Async XLA Ops:
  252.6 4.0 %copy-start = (bf16[24,128,512]{2,1,0:T(8,128)(2,1)S(1)}, bf16[24,128,512]{2,1,0:T(8,128)(2,1)}, u32[]{:S(2)}) copy-start(bf16[24,128,512]{2,1,0:T(8,128)(2,1)} %get-tuple-element.11) | copy-start | bytes 9437188
  256.7 1.7 copy-start.1

commit v3 on v2

--- a/solution.py
+++ b/solution.py
@@ -3,6 +3,7 @@
 
 import jax
 import jax.numpy as jnp
+import numpy as np
 from jax import lax
 from jax.experimental import pallas as pl
 from jax.experimental.pallas import tpu as pltpu
@@ -106,12 +107,13 @@
 
 CHUNKS = 2
 GROUP = 4
+PIECES = 2
 MESH = pl.DeviceIdType.MESH
 
 
 def kernel(
     n, direct, onset, fwd, inv, refl, fp, fm, corr,
-    ref_t, stage, zs, zr, ys, yr, rs, rr, own, minus, green, rows, cs, cr,
+    ref_t, stage, zs, zr, ys, yr, rs, rr, own, minus, green, rows, edges, cs, cr,
     load_sem, z_send, z_recv, y_send, y_recv, r_send, r_recv, c_send, c_recv,
 ):
     me = lax.axis_index("freq")
@@ -145,8 +147,7 @@
     load(1).start()
 
     def exchange(src, dst, send, recv, k):
-        o = n // 2 + k
-        off = o - (n - 1) * (o // n)
+        off = k + 1
         peer = lax.rem(me + off, n)
         return pltpu.make_async_remote_copy(
             src_ref=src.at[peer],
@@ -194,8 +195,8 @@
     def z_ops(p, c):
         return zs.at[p, c], zr.at[p, c], z_send.at[p, c], z_recv.at[p, c]
 
-    def y_ops(p, c):
-        return ys.at[p, c], yr.at[p, c], y_send.at[p, c], y_recv.at[p, c]
+    def y_ops(p, c, h):
+        return ys.at[p, c, h], yr.at[p, c, h], y_send.at[p, c, h], y_recv.at[p, c, h]
 
     def half_copy(p, c, f):
         return pltpu.make_async_remote_copy(
@@ -232,11 +233,9 @@
 
         lax.fori_loop(0, groups, step, 0)
 
-    def unpack(src):
-        size = traces * bins
-
+    def unpack(src, offset, size, stride):
         def step(j, carry):
-            rows[pl.ds(pl.multiple_of(j * size, size), size), :] = (
+            rows[pl.ds(pl.multiple_of(offset + j * stride, size), size), :] = (
                 src[j].astype(f32).reshape(size, lanes)
             )
             return carry
@@ -244,8 +243,11 @@
         lax.fori_loop(0, n, step, 0)
 
     def back(p, c):
-        wait_all(y_ops(p, c))
-        unpack(yr.at[p, c])
+        whole = traces * bins
+        piece = whole // PIECES
+        for h in range(PIECES):
+            wait_all(y_ops(p, c, h))
+            unpack(yr.at[p, c, h], h * piece, piece, whole)
         cols = slice(c * width, (c + 1) * width)
 
         def step(g, carry):
@@ -256,8 +258,9 @@
             lhs = jnp.concatenate(parts, axis=0).astype(bf16)
             out = jnp.dot(lhs, inv[...], preferred_element_type=f32)
             size = GROUP * width
-            edge = onset[c, pl.ds(pl.multiple_of(g * size, size), size), :]
-            sample = lax.broadcasted_iota(jnp.int32, out.shape, 1)
+            edge = edges[c, pl.ds(pl.multiple_of(g * size, size), size), :]
+            edge = jnp.concatenate([edge] * (samples // points), axis=1)
+            sample = lax.broadcasted_iota(jnp.int32, out.shape, 1).astype(f32)
             out = jnp.where(sample < edge, out, 0.0)
             at = pl.ds(g * GROUP, GROUP)
             if p == 0:
@@ -275,7 +278,7 @@
 
     def apply(p, c, sign):
         wait_all(z_ops(p, c))
-        unpack(zr.at[p, c])
+        unpack(zr.at[p, c], 0, traces * bins, traces * bins)
 
         def step(f, carry):
             x = rows[pl.ds(f, sources, stride=bins), :]
@@ -295,18 +298,22 @@
         lax.fori_loop(0, bins, step, 0)
 
     def reduce(p, c):
-        def step(f, carry):
-            half_copy(p, c, f).wait_recv()
-            total = own[c, f].astype(f32) + rr[p, c, f].astype(f32)
+        part = bins // PIECES
+        for h in range(PIECES):
+
+            def step(k, carry):
+                f = h * part + k
+                half_copy(p, c, f).wait_recv()
+                total = own[c, f].astype(f32) + rr[p, c, f].astype(f32)
+                if p < 2:
+                    ys[p, c, h, :, k] = total.reshape(n, traces, lanes).astype(bf16)
+                else:
+                    green[c, f] = (total - minus[c, f].astype(f32)).astype(bf16)
+                return carry
+
+            lax.fori_loop(0, part, step, 0)
             if p < 2:
-                ys[p, c, :, f] = total.reshape(n, traces, lanes).astype(bf16)
-            else:
-                green[c, f] = (total - minus[c, f].astype(f32)).astype(bf16)
-            return carry
-
-        lax.fori_loop(0, bins, step, 0)
-        if p < 2:
-            send_all(y_ops(p, c))
+                send_all(y_ops(p, c, h))
 
     def transpose(f, carry):
         load(f).wait()
@@ -320,12 +327,22 @@
 
         return carry
 
+    def columns(s, carry):
+        row = onset[pl.ds(s, 1), :].astype(f32)
+        turned = jnp.broadcast_to(row, (points, points)).T
+        for c in range(CHUNKS):
+            at = pl.ds(pl.multiple_of(s * width, width), width)
+            edges[c, at, :] = turned[c * width : (c + 1) * width]
+        return carry
+
     first(0)
     pl.semaphore_wait(barrier, n)
     send_all(z_ops(0, 0))
     first(1)
+    lax.fori_loop(0, traces, columns, 0)
+    lax.fori_loop(0, bins, transpose, 0)
+    drain_all(z_ops(0, 0))
     send_all(z_ops(0, 1))
-    lax.fori_loop(0, bins, transpose, 0)
     apply(0, 0, 1)
     reduce(0, 0)
     apply(0, 1, 1)
@@ -374,7 +391,8 @@
 
     for c in range(CHUNKS):
         for p in range(3):
-            drain_all(z_ops(p, c))
+            if (p, c) != (0, 0):
+                drain_all(z_ops(p, c))
 
             def drain(f, carry):
                 half_copy(p, c, f).wait_send()
@@ -382,7 +400,8 @@
 
             lax.fori_loop(0, bins, drain, 0)
         for p in range(2):
-            drain_all(y_ops(p, c))
+            for h in range(PIECES):
+                drain_all(y_ops(p, c, h))
 
     def drain_corr(f, carry):
         corr_copy(f).wait_send()
@@ -397,11 +416,11 @@
     _, bins, sources, receivers = reflection.shape
     width = points // CHUNKS
     frequencies = bins * n
-    forward, inverse = lookup_tables(samples, frequencies)
-    forward = forward.reshape(samples, 2 * frequencies)
-    inverse = inverse.reshape(2 * frequencies, samples)
-    edges = onset.reshape(traces, CHUNKS, width).transpose(1, 0, 2)
-    edges = edges.reshape(CHUNKS, traces * width, 1)
+    phase = np.arange(samples)[:, None] * np.arange(frequencies)[None, :] % samples
+    angles = np.float32(2.0 * math.pi / samples) * phase.astype(np.float32)
+    waves = np.concatenate([np.cos(angles), -np.sin(angles)], axis=1)
+    forward = (waves / np.float32(math.sqrt(samples))).astype(jnp.bfloat16)
+    inverse = (waves.T * np.float32(2.0 / math.sqrt(samples))).astype(jnp.bfloat16)
     bf16, dma = jnp.bfloat16, pltpu.SemaphoreType.DMA
     lanes = 2 * width
     vmem = pl.BlockSpec(memory_space=pltpu.VMEM)
@@ -419,21 +438,22 @@
             pltpu.VMEM((2, 2, sources, receivers), bf16),
             pltpu.VMEM((3, CHUNKS, n, traces, bins, lanes), bf16),
             pltpu.VMEM((3, CHUNKS, n, traces, bins, lanes), bf16),
-            pltpu.VMEM((2, CHUNKS, n, bins, traces, lanes), bf16),
-            pltpu.VMEM((2, CHUNKS, n, bins, traces, lanes), bf16),
+            pltpu.VMEM((2, CHUNKS, PIECES, n, bins // PIECES, traces, lanes), bf16),
+            pltpu.VMEM((2, CHUNKS, PIECES, n, bins // PIECES, traces, lanes), bf16),
             pltpu.VMEM((3, CHUNKS, bins, sources, lanes), bf16),
             pltpu.VMEM((3, CHUNKS, bins, sources, lanes), bf16),
             pltpu.VMEM((CHUNKS, bins, sources, lanes), bf16),
             pltpu.VMEM((CHUNKS, bins, sources, lanes), bf16),
             pltpu.VMEM((CHUNKS, bins, sources, lanes), bf16),
             pltpu.VMEM((n * traces * bins, lanes), jnp.float32),
+            pltpu.VMEM((CHUNKS, traces * width, points), jnp.float32),
             pltpu.VMEM((2, bins, 2, points // 2, points), bf16),
             pltpu.VMEM((bins, 2, points // 2, points), bf16),
             dma((2,)),
             dma((3, CHUNKS, n)),
             dma((3, CHUNKS, n)),
-            dma((2, CHUNKS, n)),
-            dma((2, CHUNKS, n)),
+            dma((2, CHUNKS, PIECES, n)),
+            dma((2, CHUNKS, PIECES, n)),
             dma((3, CHUNKS, bins)),
             dma((3, CHUNKS, bins)),
             dma((bins,)),
@@ -442,7 +462,7 @@
         compiler_params=pltpu.CompilerParams(
             collective_id=0, has_side_effects=True, vmem_limit_bytes=67043328
         ),
-    )(direct, edges, forward, inverse, reflection)
+    )(direct, onset, jnp.asarray(forward), jnp.asarray(inverse), reflection)
 
 
 def fits(reflection, direct):

time: 259 us -> 241 us (0.931); the launches traced: 259 us -> 238 us
  Pallas kernels: 245 us -> 230 us
  other arithmetic: 3.59 us -> 0 us
  local copies, waits for them, and re-layouts: 9.96 us -> 6.47 us
    pallas_call x1, Pallas kernels: 245 us -> 230 us  [fused(): pl.pallas_call(functools.partial(kernel, n), out_shape=(jax.ShapeDtypeStr...]
    reshape x3 -> x0, local copies, waits for them, and re-layouts: 3.49 us -> none  [the longest x1 2.69 us: fused(): edges = edges.reshape(CHUNKS, traces * width, 1)]
where the time goes in v3:
time: 241 us; the launch traced here: 238 us
  Pallas kernels  230 us (95%)
  local copies, waits for them, and re-layouts  6.47 us (3%)
    pallas_call x1, Pallas kernels, fused(): pl.pallas_call(functools.partial(kernel, n), out_shape=(jax.ShapeDtypeStr...  230 us
    unnamed x7, local copies, waits for them, and re-layouts  6.47 us

profile of v3, /device:TPU:28, one launch (start us, length us, event | category | flops | bytes accessed | tf_op | source)
XLA Modules:
  0.0 237.6 jit_solution(6407961997544994501)
XLA Ops:
  0.6 230.5 %shard_map.76 = (bf16[24,128,512]{2,1,0:T(8,128)(2,1)}, bf16[24,128,512]{2,1,0:T(8,128)(2,1)}, f32[2,8,64,128]{3,2,1,0:T(8,128)}) custom-call(bf16[24,128,512]{2,1,0:T(8,128)(2,1)} %direct.1, s32[24,128]{1,0:T(8,128)} %onset.1, bf16[512,256]{1,0:T(8,128)(2,1)} %constant.4.clone.fwd, bf16[256,512]{1,0:T(8,128)(2,1)} %constant.5.clone.inv, ...), custom_call_target="tpu_custom_call" | custom-call | tf_op jit(solution)/shard_map/pallas_call | solution.py:427
  231.1 0.0 copy-start
  231.1 4.0 %copy.11 = bf16[24,128,512]{2,1,0:T(8,128)(2,1)} copy(bf16[24,128,512]{2,1,0:T(8,128)(2,1)} %get-tuple-element.6) | data formatting | bytes 6291456
  235.1 0.0 copy-done
  235.1 0.0 copy-start.1
  235.1 1.7 copy.12
  236.8 0.0 copy-done.1
  236.8 0.8 copy.13
Async XLA Ops:
  231.1 4.0 %copy-start = (bf16[24,128,512]{2,1,0:T(8,128)(2,1)S(1)}, bf16[24,128,512]{2,1,0:T(8,128)(2,1)}, u32[]{:S(2)}) copy-start(bf16[24,128,512]{2,1,0:T(8,128)(2,1)} %get-tuple-element.7) | copy-start | bytes 9437188
  235.1 1.7 copy-start.1

commit v4 on v3

--- a/solution.py
+++ b/solution.py
@@ -297,9 +297,9 @@
 
         lax.fori_loop(0, bins, step, 0)
 
-    def reduce(p, c):
+    def reduce(p, c, pieces=range(PIECES)):
         part = bins // PIECES
-        for h in range(PIECES):
+        for h in pieces:
 
             def step(k, carry):
                 f = h * part + k
@@ -344,20 +344,22 @@
     drain_all(z_ops(0, 0))
     send_all(z_ops(0, 1))
     apply(0, 0, 1)
-    reduce(0, 0)
+    reduce(0, 0, range(PIECES - 1))
     apply(0, 1, 1)
+    reduce(0, 0, range(PIECES - 1, PIECES))
     reduce(0, 1)
     back(0, 0)
     back(0, 1)
     apply(1, 0, -1)
-    reduce(1, 0)
+    reduce(1, 0, range(PIECES - 1))
     apply(1, 1, -1)
+    reduce(1, 0, range(PIECES - 1, PIECES))
     reduce(1, 1)
     back(1, 0)
     back(1, 1)
     apply(2, 0, 1)
+    apply(2, 1, 1)
     reduce(2, 0)
-    apply(2, 1, 1)
     reduce(2, 1)
 
     half = points // 2

time: 241 us -> 233 us (0.967)
  Pallas kernels: 230 us -> 225 us
    pallas_call x1, Pallas kernels: 230 us -> 225 us  [fused(): pl.pallas_call(functools.partial(kernel, n), out_shape=(jax.ShapeDtypeStr...]
where the time goes in v4:
time: 233 us; the launch traced here: 232 us
  Pallas kernels  225 us (97%)
  local copies, waits for them, and re-layouts  6.47 us (3%)
    pallas_call x1, Pallas kernels, fused(): pl.pallas_call(functools.partial(kernel, n), out_shape=(jax.ShapeDtypeStr...  225 us
    unnamed x7, local copies, waits for them, and re-layouts  6.47 us

profile of v4, /device:TPU:28, one launch (start us, length us, event | category | flops | bytes accessed | tf_op | source)
XLA Modules:
  0.0 231.7 jit_solution(2149773132504224999)
XLA Ops:
  0.6 224.5 %shard_map.76 = (bf16[24,128,512]{2,1,0:T(8,128)(2,1)}, bf16[24,128,512]{2,1,0:T(8,128)(2,1)}, f32[2,8,64,128]{3,2,1,0:T(8,128)}) custom-call(bf16[24,128,512]{2,1,0:T(8,128)(2,1)} %direct.1, s32[24,128]{1,0:T(8,128)} %onset.1, bf16[512,256]{1,0:T(8,128)(2,1)} %constant.4.clone.fwd, bf16[256,512]{1,0:T(8,128)(2,1)} %constant.5.clone.inv, ...), custom_call_target="tpu_custom_call" | custom-call | tf_op jit(solution)/shard_map/pallas_call | solution.py:429
  225.2 0.0 copy-start
  225.2 4.0 %copy.11 = bf16[24,128,512]{2,1,0:T(8,128)(2,1)} copy(bf16[24,128,512]{2,1,0:T(8,128)(2,1)} %get-tuple-element.6) | data formatting | bytes 6291456
  229.2 0.0 copy-done
  229.2 0.0 copy-start.1
  229.2 1.7 copy.12
  230.9 0.0 copy-done.1
  230.9 0.8 copy.13
Async XLA Ops:
  225.2 4.0 %copy-start = (bf16[24,128,512]{2,1,0:T(8,128)(2,1)S(1)}, bf16[24,128,512]{2,1,0:T(8,128)(2,1)}, u32[]{:S(2)}) copy-start(bf16[24,128,512]{2,1,0:T(8,128)(2,1)} %get-tuple-element.7) | copy-start | bytes 9437188
  229.2 1.7 copy-start.1
